TPU v7x, 128 devices: a whole 4x4x4 slice. The times are simulated.
128 devices in a mesh: patch: 16 (over y, x), col: 8 (over z, core).
Axes of the slice: x: 4, y: 4, z: 4, core: 2. Of those that a mesh axis runs over, the one named last changes fastest.
Arguments:
- potential0: float32 [512, 16, 128], P(('patch', 'col')), may hold values from -3 to 3
- source_term: float32 [512, 16, 128], P(('patch', 'col')), may hold values from -9 to 9
- self_coef: float32 [512, 128], P(('patch', 'col')), may hold values from 1 to 4
- nearfield: float32 [512, 24, 128, 128], P(('patch', 'col')), may hold values from -0.109375 to 0.109375
- precond: float32 [512, 128, 128], P(('patch', 'col')), may hold values from -1 to 2
- exch_current: float32 [512, 128], P(('patch', 'col')), may hold values from 0.05 to 0.5
- conductance: float32 [512, 128], P(('patch', 'col')), may hold values from 0.1 to 1
- member: int32 [512, 128], P(('patch', 'col')), may hold values from 0 to 63
- anode_drive: float32 [64], replicated, may hold values from -1 to 1
- pair_source: int32 [512, 24], P(('patch', 'col')), may hold values from 0 to 39
- pair_count: int32 [512], P(('patch', 'col')), may hold values from 1 to 24, as said below
Outputs:
- potential: float32 [512, 16, 128], P(('patch', 'col'))
- residual: float32 [512, 16, 128], P(('patch', 'col'))
Inputs may be any that keep to these rules, and one draw needn't show every extreme that they name: Slots k < pair_count[b] of block b are live; some block has all 24 slots live, and the blocks of some devices hold far more live pairs than those of others.
All inputs are finite; a program needn't handle non-finite values.
Results may differ from a plain program's by a relative error of at most 0.0003.
Values sent between devices are 32-bit elements; how exact they have to be, the bound alone decides.
A program may use at most 64 MiB of HBM per device.

v0:
```python
import jax
import jax.numpy as jnp
from jax import lax
from jax.sharding import PartitionSpec as P

NEWTON = 2
GMRES = 2
ALPHA = 0.6
BETA = 0.4
EPS = 1e-06


def from_behind(array, axis, by):
    size = lax.axis_size(axis)
    return lax.ppermute(array, axis, [(i, (i + by) % size) for i in range(size)])


def column_sum(left, right):
    return jnp.sum(left * right, axis=(0, 2))


def least_squares(columns, beta):
    depth = len(columns)
    hessen = jnp.zeros((beta.shape[0], depth + 1, depth), jnp.float32)
    for place in range(depth):
        hessen = hessen.at[:, : place + 2, place].set(columns[place].T)
    gram = jnp.einsum("cij,cik->cjk", hessen, hessen, precision=lax.Precision.HIGHEST)
    right = beta[:, None] * hessen[:, 0, :]
    lower = jnp.linalg.cholesky(gram)
    middle = jax.scipy.linalg.solve_triangular(lower, right[:, :, None], lower=True)
    return jax.scipy.linalg.solve_triangular(lower, middle, lower=True, trans=1)[:, :, 0]


def body(
    potential0,
    source_term,
    self_coef,
    nearfield,
    precond,
    exch_current,
    conductance,
    member,
    anode_drive,
    pair_source,
    pair_count,
):
    pair_slots = pair_source.shape[1]
    live_mask = (jnp.arange(pair_slots, dtype=jnp.int32)[None, :] < pair_count[:, None]).astype(
        jnp.float32
    )
    members = anode_drive.shape[0]
    onehot = (jnp.arange(members, dtype=jnp.int32)[:, None, None] == member[None]).astype(
        jnp.float32
    )
    member_drive = jnp.sum(onehot * anode_drive[:, None, None], axis=0)
    diagonal = self_coef[:, None, :]
    current = exch_current[:, None, :]
    conduct = conductance[:, None, :]

    def near_field(field):
        own_patch = lax.all_gather(field, "col", axis=0, tiled=True)
        before = from_behind(field, "patch", 1)
        following = from_behind(field, "patch", -1)
        stacked = jnp.concatenate([own_patch, before, following], axis=0)
        sources = stacked[pair_source]
        return jnp.einsum(
            "bkij,bkcj->bci",
            nearfield,
            sources * live_mask[:, :, None, None],
            precision=lax.Precision.HIGHEST,
        )

    def mismatch(field, near_value):
        grow = jnp.exp(ALPHA * field)
        shrink = jnp.exp(-BETA * field)
        value = (
            diagonal * field
            + near_value
            + current * (grow - shrink)
            + conduct * (field - member_drive[:, None, :])
            - source_term
        )
        slope = current * (ALPHA * grow + BETA * shrink) + conduct
        return (value, slope)

    field = potential0
    near_now = near_field(field)
    for newton in range(NEWTON):
        value, slope = mismatch(field, near_now)
        start = -value
        beta = jnp.sqrt(lax.psum(column_sum(start, start), ("patch", "col")) + EPS)
        basis = [start / beta[None, :, None]]
        directions = []
        near_images = []
        columns = []
        for step in range(GMRES):
            direction = jnp.einsum(
                "bij,bcj->bci", precond, basis[step], precision=lax.Precision.HIGHEST
            )
            directions.append(direction)
            near_image = near_field(direction)
            near_images.append(near_image)
            image = diagonal * direction + near_image + slope * direction
            coeffs = []
            for place in range(step + 1):
                coeff = lax.psum(column_sum(basis[place], image), ("patch", "col"))
                image = image - coeff[None, :, None] * basis[place]
                coeffs.append(coeff)
            norm = jnp.sqrt(lax.psum(column_sum(image, image), ("patch", "col")) + EPS)
            basis.append(image / norm[None, :, None])
            columns.append(jnp.stack(coeffs + [norm]))
        weights = least_squares(columns, beta)
        update = jnp.zeros_like(field)
        for step in range(GMRES):
            update = update + weights[:, step][None, :, None] * directions[step]
        field = field + update
        near_now = near_field(field)
    final_value, final_slope = mismatch(field, near_now)
    return (field, final_value)


def solution(mesh):
    return jax.shard_map(
        body,
        mesh=mesh,
        in_specs=(
            P(("patch", "col"), None, None),
            P(("patch", "col"), None, None),
            P(("patch", "col"), None),
            P(("patch", "col"), None, None, None),
            P(("patch", "col"), None, None),
            P(("patch", "col"), None),
            P(("patch", "col"), None),
            P(("patch", "col"), None),
            P(),
            P(("patch", "col"), None),
            P(("patch", "col")),
        ),
        out_specs=(P(("patch", "col"), None, None), P(("patch", "col"), None, None)),
        check_vma=False,
    )
```

profile of v0, /device:TPU:1, one launch (start us, length us, event | category | flops | bytes accessed | tf_op | source)
XLA Modules:
  0.0 974.0 jit_solution(4111155873102971596)
XLA Ops:
  2.8 3.8 collective-permute-start.1
  6.6 15.1 %all_gather.21 = f32[32,16,128]{2,1,0:T(8,128)S(1)} all-gather(f32[4,16,128]{2,1,0:T(8,128)} %param.24), channel_id=1, replica_groups=mesh['patch'=16,'col'=8] {'col'}, dimensions={0}, use_global_device_ids=true | all-gather | bytes 294912 | tf_op jit(solution)/shard_map/all_gather | solution.py:61
  24.7 7.6 multiply_reduce_fusion.11
  32.3 64.2 %psum.84 = f32[16]{0:T(128)S(1)} all-reduce(f32[16]{0:T(128)S(1)} %get-tuple-element.61), channel_id=1, replica_groups=mesh['patch'=16,'col'=8] {'patch','col'}, use_global_device_ids=true, to_apply=%region_2.0 | all-reduce | flops 16 | bytes 128 | tf_op jit(solution)/shard_map/psum | solution.py:91
  97.3 4.6 collective-permute-start.3
  101.9 13.9 %all_gather.22 = f32[32,16,128]{2,1,0:T(8,128)S(1)} all-gather(f32[4,16,128]{2,1,0:T(8,128)S(1)} %fusion.43), channel_id=1, replica_groups=mesh['patch'=16,'col'=8] {'col'}, dimensions={0}, use_global_device_ids=true | all-gather | bytes 294912 | tf_op jit(solution)/shard_map/all_gather | solution.py:61
  116.5 7.5 multiply_reduce_fusion.10
  124.0 63.4 %psum.85 = f32[16]{0:T(128)S(1)} all-reduce(f32[16]{0:T(128)S(1)} %get-tuple-element.63), channel_id=1, replica_groups=mesh['patch'=16,'col'=8] {'patch','col'}, use_global_device_ids=true, to_apply=%region_4.0 | all-reduce | flops 16 | bytes 128 | tf_op jit(solution)/shard_map/psum | solution.py:106
  187.6 63.0 %psum.86 = f32[16]{0:T(128)S(1)} all-reduce(f32[16]{0:T(128)S(1)} %multiply_reduce_fusion.9), channel_id=1, replica_groups=mesh['patch'=16,'col'=8] {'patch','col'}, use_global_device_ids=true, to_apply=%region_6.0 | all-reduce | flops 16 | bytes 128 | tf_op jit(solution)/shard_map/psum | solution.py:109
  252.1 4.0 collective-permute-start.5
  256.0 13.8 %all_gather.23 = f32[32,16,128]{2,1,0:T(8,128)S(1)} all-gather(f32[4,16,128]{2,1,0:T(8,128)S(1)} %fusion.44), channel_id=1, replica_groups=mesh['patch'=16,'col'=8] {'col'}, dimensions={0}, use_global_device_ids=true | all-gather | bytes 294912 | tf_op jit(solution)/shard_map/all_gather | solution.py:61
  270.5 7.5 multiply_reduce_fusion.8
  278.0 64.4 %psum.87 = f32[16]{0:T(128)S(1)} all-reduce(f32[16]{0:T(128)S(1)} %get-tuple-element.65), channel_id=1, replica_groups=mesh['patch'=16,'col'=8] {'patch','col'}, use_global_device_ids=true, to_apply=%region_8.0 | all-reduce | flops 16 | bytes 128 | tf_op jit(solution)/shard_map/psum | solution.py:106
  342.6 62.5 %psum.88 = f32[16]{0:T(128)S(1)} all-reduce(f32[16]{0:T(128)S(1)} %multiply_reduce_fusion.7), channel_id=1, replica_groups=mesh['patch'=16,'col'=8] {'patch','col'}, use_global_device_ids=true, to_apply=%region_10.0 | all-reduce | flops 16 | bytes 128 | tf_op jit(solution)/shard_map/psum | solution.py:106
  405.3 64.0 %psum.89 = f32[16]{0:T(128)S(1)} all-reduce(f32[16]{0:T(128)S(1)} %multiply_reduce_fusion.6), channel_id=1, replica_groups=mesh['patch'=16,'col'=8] {'patch','col'}, use_global_device_ids=true, to_apply=%region_12.0 | all-reduce | flops 16 | bytes 128 | tf_op jit(solution)/shard_map/psum | solution.py:109
  476.7 4.8 collective-permute-start.7
  481.5 14.5 %all_gather.24 = f32[32,16,128]{2,1,0:T(8,128)S(1)} all-gather(f32[4,16,128]{2,1,0:T(8,128)S(1)} %add_add_fusion.1), channel_id=1, replica_groups=mesh['patch'=16,'col'=8] {'col'}, dimensions={0}, use_global_device_ids=true | all-gather | bytes 294912 | tf_op jit(solution)/shard_map/all_gather | solution.py:61
  496.7 7.5 multiply_reduce_fusion.5
  504.2 61.8 %psum.90 = f32[16]{0:T(128)S(1)} all-reduce(f32[16]{0:T(128)S(1)} %get-tuple-element.67), channel_id=1, replica_groups=mesh['patch'=16,'col'=8] {'patch','col'}, use_global_device_ids=true, to_apply=%region_16.0 | all-reduce | flops 16 | bytes 128 | tf_op jit(solution)/shard_map/psum | solution.py:91
  571.4 13.9 %all_gather.25 = f32[32,16,128]{2,1,0:T(8,128)S(1)} all-gather(f32[4,16,128]{2,1,0:T(8,128)S(1)} %fusion.45), channel_id=1, replica_groups=mesh['patch'=16,'col'=8] {'col'}, dimensions={0}, use_global_device_ids=true | all-gather | bytes 294912 | tf_op jit(solution)/shard_map/all_gather | solution.py:61
  586.0 7.5 multiply_reduce_fusion.4
  593.5 63.5 %psum.91 = f32[16]{0:T(128)S(1)} all-reduce(f32[16]{0:T(128)S(1)} %get-tuple-element.69), channel_id=1, replica_groups=mesh['patch'=16,'col'=8] {'patch','col'}, use_global_device_ids=true, to_apply=%region_18.0 | all-reduce | flops 16 | bytes 128 | tf_op jit(solution)/shard_map/psum | solution.py:106
  657.1 62.6 %psum.92 = f32[16]{0:T(128)S(1)} all-reduce(f32[16]{0:T(128)S(1)} %multiply_reduce_fusion.3), channel_id=1, replica_groups=mesh['patch'=16,'col'=8] {'patch','col'}, use_global_device_ids=true, to_apply=%region_20.0 | all-reduce | flops 16 | bytes 128 | tf_op jit(solution)/shard_map/psum | solution.py:109
  721.1 4.0 collective-permute-start.11
  725.0 14.0 %all_gather.26 = f32[32,16,128]{2,1,0:T(8,128)S(1)} all-gather(f32[4,16,128]{2,1,0:T(8,128)S(1)} %fusion.46), channel_id=1, replica_groups=mesh['patch'=16,'col'=8] {'col'}, dimensions={0}, use_global_device_ids=true | all-gather | bytes 294912 | tf_op jit(solution)/shard_map/all_gather | solution.py:61
  739.8 7.5 multiply_reduce_fusion.2
  747.2 64.4 %psum.93 = f32[16]{0:T(128)S(1)} all-reduce(f32[16]{0:T(128)S(1)} %get-tuple-element.71), channel_id=1, replica_groups=mesh['patch'=16,'col'=8] {'patch','col'}, use_global_device_ids=true, to_apply=%region_22.0 | all-reduce | flops 16 | bytes 128 | tf_op jit(solution)/shard_map/psum | solution.py:106
  811.8 62.5 %psum.94 = f32[16]{0:T(128)S(1)} all-reduce(f32[16]{0:T(128)S(1)} %multiply_reduce_fusion.1), channel_id=1, replica_groups=mesh['patch'=16,'col'=8] {'patch','col'}, use_global_device_ids=true, to_apply=%region_24.0 | all-reduce | flops 16 | bytes 128 | tf_op jit(solution)/shard_map/psum | solution.py:106
  874.5 64.0 %psum.95 = f32[16]{0:T(128)S(1)} all-reduce(f32[16]{0:T(128)S(1)} %multiply_reduce_fusion), channel_id=1, replica_groups=mesh['patch'=16,'col'=8] {'patch','col'}, use_global_device_ids=true, to_apply=%region_26.0 | all-reduce | flops 16 | bytes 128 | tf_op jit(solution)/shard_map/psum | solution.py:109
  946.0 4.8 collective-permute-start.13
  950.8 14.3 %all_gather.27 = f32[32,16,128]{2,1,0:T(8,128)S(1)} all-gather(f32[4,16,128]{2,1,0:T(8,128)S(1)} %add_add_fusion), channel_id=1, replica_groups=mesh['patch'=16,'col'=8] {'col'}, dimensions={0}, use_global_device_ids=true | all-gather | bytes 294912 | tf_op jit(solution)/shard_map/all_gather | solution.py:61
  965.8 8.0 fusion.3
  (115 shorter events, 34.3 us)
Async XLA Ops:
  0.6 95.9 %copy-start = (f32[4,128,128]{2,1,0:T(8,128)S(1)}, f32[4,128,128]{2,1,0:T(8,128)}, u32[]{:S(2)}) copy-start(f32[4,128,128]{2,1,0:T(8,128)} %param.28) | copy-start | bytes 786436
  0.6 115.9 %copy-start.1 = (f32[4,16,128]{2,1,0:T(8,128)S(1)}, f32[4,16,128]{2,1,0:T(8,128)}, u32[]{:S(2)}) copy-start(f32[4,16,128]{2,1,0:T(8,128)} %param.24) | copy-start | bytes 98308
  0.7 115.9 %copy-start.6 = (f32[4,128]{1,0:T(4,128)S(1)}, f32[4,128]{1,0:T(4,128)}, u32[]{:S(2)}) copy-start(f32[4,128]{1,0:T(4,128)} %param.26) | copy-start | bytes 6148
  0.7 115.9 %copy-start.5 = (f32[4,128]{1,0:T(4,128)S(1)}, f32[4,128]{1,0:T(4,128)}, u32[]{:S(2)}) copy-start(f32[4,128]{1,0:T(4,128)} %param.29) | copy-start | bytes 6148
  0.7 115.9 %copy-start.4 = (f32[4,128]{1,0:T(4,128)S(1)}, f32[4,128]{1,0:T(4,128)}, u32[]{:S(2)}) copy-start(f32[4,128]{1,0:T(4,128)} %param.30) | copy-start | bytes 6148
  0.7 23.3 %collective-permute-start = (f32[4,16,128]{2,1,0:T(8,128)}, f32[4,16,128]{2,1,0:T(8,128)S(1)}, u32[]{:S(2)}, u32[]{:S(2)}) collective-permute-start(f32[4,16,128]{2,1,0:T(8,128)} %param.24), channel_id=1, source_target_pairs={{0,8},{8,16},{16,24},{24,32},{32,40},{40,48},{48,56},{56,64},{64,7... | collective-permute-start | bytes 98312 | tf_op jit(solution)/shard_map/ppermute | solution.py:15
  2.8 21.2 %collective-permute-start.1 = (f32[4,16,128]{2,1,0:T(8,128)}, f32[4,16,128]{2,1,0:T(8,128)S(1)}, u32[]{:S(2)}, u32[]{:S(2)}) collective-permute-start(f32[4,16,128]{2,1,0:T(8,128)} %param.24), channel_id=1, source_target_pairs={{0,120},{8,0},{16,8},{24,16},{32,24},{40,32},{48,40},{56,48},{64,5... | collective-permute-start | bytes 98312 | tf_op jit(solution)/shard_map/ppermute | solution.py:15
  97.1 18.7 %collective-permute-start.2 = (f32[4,16,128]{2,1,0:T(8,128)S(1)}, f32[4,16,128]{2,1,0:T(8,128)S(1)}, u32[]{:S(2)}, u32[]{:S(2)}) collective-permute-start(f32[4,16,128]{2,1,0:T(8,128)S(1)} %fusion.43), channel_id=1, source_target_pairs={{0,8},{8,16},{16,24},{24,32},{32,40},{40,48},{48,56},{56,64},{64,7... | collective-permute-start | bytes 98312 | tf_op jit(solution)/shard_map/ppermute | solution.py:15
  97.3 18.4 %collective-permute-start.3 = (f32[4,16,128]{2,1,0:T(8,128)S(1)}, f32[4,16,128]{2,1,0:T(8,128)S(1)}, u32[]{:S(2)}, u32[]{:S(2)}) collective-permute-start(f32[4,16,128]{2,1,0:T(8,128)S(1)} %fusion.43), channel_id=1, source_target_pairs={{0,120},{8,0},{16,8},{24,16},{32,24},{40,32},{48,40},{56,48},{64,5... | collective-permute-start | bytes 98312 | tf_op jit(solution)/shard_map/ppermute | solution.py:15
  251.2 18.6 %collective-permute-start.4 = (f32[4,16,128]{2,1,0:T(8,128)S(1)}, f32[4,16,128]{2,1,0:T(8,128)S(1)}, u32[]{:S(2)}, u32[]{:S(2)}) collective-permute-start(f32[4,16,128]{2,1,0:T(8,128)S(1)} %fusion.44), channel_id=1, source_target_pairs={{0,8},{8,16},{16,24},{24,32},{32,40},{40,48},{48,56},{56,64},{64,7... | collective-permute-start | bytes 98312 | tf_op jit(solution)/shard_map/ppermute | solution.py:15
  252.1 17.7 %collective-permute-start.5 = (f32[4,16,128]{2,1,0:T(8,128)S(1)}, f32[4,16,128]{2,1,0:T(8,128)S(1)}, u32[]{:S(2)}, u32[]{:S(2)}) collective-permute-start(f32[4,16,128]{2,1,0:T(8,128)S(1)} %fusion.44), channel_id=1, source_target_pairs={{0,120},{8,0},{16,8},{24,16},{32,24},{40,32},{48,40},{56,48},{64,5... | collective-permute-start | bytes 98312 | tf_op jit(solution)/shard_map/ppermute | solution.py:15
  269.8 226.9 %copy-start.2 = (f32[4,16,128]{2,1,0:T(8,128)S(1)}, f32[4,16,128]{2,1,0:T(8,128)}, u32[]{:S(2)}) copy-start(f32[4,16,128]{2,1,0:T(8,128)} %param.25) | copy-start | bytes 98308
  476.7 19.3 %collective-permute-start.6 = (f32[4,16,128]{2,1,0:T(8,128)S(1)}, f32[4,16,128]{2,1,0:T(8,128)S(1)}, u32[]{:S(2)}, u32[]{:S(2)}) collective-permute-start(f32[4,16,128]{2,1,0:T(8,128)S(1)} %add_add_fusion.1), channel_id=1, source_target_pairs={{0,8},{8,16},{16,24},{24,32},{32,40},{40,48},{48,56},{56,64},{64,7... | collective-permute-start | bytes 98312 | tf_op jit(solution)/shard_map/ppermute | solution.py:15
  476.7 19.3 %collective-permute-start.7 = (f32[4,16,128]{2,1,0:T(8,128)S(1)}, f32[4,16,128]{2,1,0:T(8,128)S(1)}, u32[]{:S(2)}, u32[]{:S(2)}) collective-permute-start(f32[4,16,128]{2,1,0:T(8,128)S(1)} %add_add_fusion.1), channel_id=1, source_target_pairs={{0,120},{8,0},{16,8},{24,16},{32,24},{40,32},{48,40},{56,48},{64,5... | collective-permute-start | bytes 98312 | tf_op jit(solution)/shard_map/ppermute | solution.py:15
  566.6 18.7 %collective-permute-start.8 = (f32[4,16,128]{2,1,0:T(8,128)S(1)}, f32[4,16,128]{2,1,0:T(8,128)S(1)}, u32[]{:S(2)}, u32[]{:S(2)}) collective-permute-start(f32[4,16,128]{2,1,0:T(8,128)S(1)} %fusion.45), channel_id=1, source_target_pairs={{0,8},{8,16},{16,24},{24,32},{32,40},{40,48},{48,56},{56,64},{64,7... | collective-permute-start | bytes 98312 | tf_op jit(solution)/shard_map/ppermute | solution.py:15
  567.7 17.5 %collective-permute-start.9 = (f32[4,16,128]{2,1,0:T(8,128)S(1)}, f32[4,16,128]{2,1,0:T(8,128)S(1)}, u32[]{:S(2)}, u32[]{:S(2)}) collective-permute-start(f32[4,16,128]{2,1,0:T(8,128)S(1)} %fusion.45), channel_id=1, source_target_pairs={{0,120},{8,0},{16,8},{24,16},{32,24},{40,32},{48,40},{56,48},{64,5... | collective-permute-start | bytes 98312 | tf_op jit(solution)/shard_map/ppermute | solution.py:15
  720.2 18.8 %collective-permute-start.10 = (f32[4,16,128]{2,1,0:T(8,128)S(1)}, f32[4,16,128]{2,1,0:T(8,128)S(1)}, u32[]{:S(2)}, u32[]{:S(2)}) collective-permute-start(f32[4,16,128]{2,1,0:T(8,128)S(1)} %fusion.46), channel_id=1, source_target_pairs={{0,8},{8,16},{16,24},{24,32},{32,40},{40,48},{48,56},{56,64},{64,7... | collective-permute-start | bytes 98312 | tf_op jit(solution)/shard_map/ppermute | solution.py:15
  721.1 17.9 %collective-permute-start.11 = (f32[4,16,128]{2,1,0:T(8,128)S(1)}, f32[4,16,128]{2,1,0:T(8,128)S(1)}, u32[]{:S(2)}, u32[]{:S(2)}) collective-permute-start(f32[4,16,128]{2,1,0:T(8,128)S(1)} %fusion.46), channel_id=1, source_target_pairs={{0,120},{8,0},{16,8},{24,16},{32,24},{40,32},{48,40},{56,48},{64,5... | collective-permute-start | bytes 98312 | tf_op jit(solution)/shard_map/ppermute | solution.py:15
  945.9 27.9 %copy-start.3 = (f32[4,16,128]{2,1,0:T(8,128)}, f32[4,16,128]{2,1,0:T(8,128)S(1)}, u32[]{:S(2)}) copy-start(f32[4,16,128]{2,1,0:T(8,128)S(1)} %add_add_fusion) | copy-start | bytes 98308
  945.9 19.2 %collective-permute-start.12 = (f32[4,16,128]{2,1,0:T(8,128)S(1)}, f32[4,16,128]{2,1,0:T(8,128)S(1)}, u32[]{:S(2)}, u32[]{:S(2)}) collective-permute-start(f32[4,16,128]{2,1,0:T(8,128)S(1)} %add_add_fusion), channel_id=1, source_target_pairs={{0,8},{8,16},{16,24},{24,32},{32,40},{40,48},{48,56},{56,64},{64,7... | collective-permute-start | bytes 98312 | tf_op jit(solution)/shard_map/ppermute | solution.py:15
  946.0 19.1 %collective-permute-start.13 = (f32[4,16,128]{2,1,0:T(8,128)S(1)}, f32[4,16,128]{2,1,0:T(8,128)S(1)}, u32[]{:S(2)}, u32[]{:S(2)}) collective-permute-start(f32[4,16,128]{2,1,0:T(8,128)S(1)} %add_add_fusion), channel_id=1, source_target_pairs={{0,120},{8,0},{16,8},{24,16},{32,24},{40,32},{48,40},{56,48},{64,5... | collective-permute-start | bytes 98312 | tf_op jit(solution)/shard_map/ppermute | solution.py:15
where the time goes:
time: 984 us; the launch traced here: 974 us
  blocking collectives  860 us (87%)
  matrix products  55.7 us (6%)
  starting transfers between devices  34.8 us (4%)
  other arithmetic  16.5 us (2%)
    psum x6, blocking collectives, body(): coeff = lax.psum(column_sum(basis[place], image), ('patch', 'col'))  381 us
    psum x4, blocking collectives, body(): norm = jnp.sqrt(lax.psum(column_sum(image, image), ('patch', 'col')) + EPS)  254 us
    psum x2, blocking collectives, body(): beta = jnp.sqrt(lax.psum(column_sum(start, start), ('patch', 'col')) + EPS)  126 us
    all_gather x7, blocking collectives, near_field(): own_patch = lax.all_gather(field, 'col', axis=0, tiled=True)  99.4 us
    dot_general x7, matrix products, near_field(): jnp.einsum('bkij,bkcj->bci', nearfield, sources * live_mask[:, :, None, N...  52.9 us
    ppermute x14, starting transfers between devices, from_behind(): lax.ppermute(array, axis, [(i, (i + by) % size) for i in range(size)])  34.8 us
  transfers between devices with their start and end apart: 14, of which 0 were waited for; matrix products, arithmetic and copies ran while one was open for 0% of the time, Pallas kernels for 0%

commit v1 on v0

--- a/solution.py
+++ b/solution.py
@@ -58,7 +58,10 @@
     conduct = conductance[:, None, :]
 
     def near_field(field):
-        own_patch = lax.all_gather(field, "col", axis=0, tiled=True)
+        devices = lax.axis_size("col")
+        parts = jnp.stack([field for _ in range(devices)])
+        parts = lax.all_to_all(parts, "col", split_axis=0, concat_axis=0)
+        own_patch = jnp.concatenate(parts, axis=0)
         before = from_behind(field, "patch", 1)
         following = from_behind(field, "patch", -1)
         stacked = jnp.concatenate([own_patch, before, following], axis=0)

time: 984 us -> 952 us (0.967)
  blocking collectives: 860 us -> 774 us
  starting transfers between devices: 34.8 us -> 66.4 us
  waiting for transfers between devices: 0.04 us -> 15.7 us
    all_gather x7 -> x0, blocking collectives: 99.4 us -> none  [near_field(): own_patch = lax.all_gather(field, 'col', axis=0, tiled=True)]
    all_to_all x0 -> x7, starting transfers between devices: none -> 31.2 us  [near_field(): parts = lax.all_to_all(parts, 'col', split_axis=0, concat_axis=0)]
    psum x6, blocking collectives: 381 us -> 391 us  [body(): coeff = lax.psum(column_sum(basis[place], image), ('patch', 'col'))]
  transfers between devices with their start and end apart: 14 -> 21, of which waited for: 0 -> 14; matrix products, arithmetic and copies ran while one was open for 0% -> 0% of each run, Pallas kernels for 0% -> 0%
where the time goes in v1:
time: 952 us; the launch traced here: 941 us
  blocking collectives  774 us (81%)
  starting transfers between devices  66.4 us (7%)
  matrix products  55.7 us (6%)
  other arithmetic  16.5 us (2%)
  waiting for transfers between devices  15.7 us (2%)
  local copies, waits for them, and re-layouts  12 us (1%)
    psum x6, blocking collectives, body(): coeff = lax.psum(column_sum(basis[place], image), ('patch', 'col'))  391 us
    psum x4, blocking collectives, body(): norm = jnp.sqrt(lax.psum(column_sum(image, image), ('patch', 'col')) + EPS)  253 us
    psum x2, blocking collectives, body(): beta = jnp.sqrt(lax.psum(column_sum(start, start), ('patch', 'col')) + EPS)  130 us
    dot_general x7, matrix products, near_field(): jnp.einsum('bkij,bkcj->bci', nearfield, sources * live_mask[:, :, None, N...  52.9 us
    ppermute x14, starting transfers between devices, from_behind(): lax.ppermute(array, axis, [(i, (i + by) % size) for i in range(size)])  35.3 us
    all_to_all x7, starting transfers between devices, near_field(): parts = lax.all_to_all(parts, 'col', split_axis=0, concat_axis=0)  31.2 us
  transfers between devices with their start and end apart: 21, of which 14 were waited for; matrix products, arithmetic and copies ran while one was open for 0% of the time, Pallas kernels for 0%

profile of v1, /device:TPU:1, one launch (start us, length us, event | category | flops | bytes accessed | tf_op | source)
XLA Modules:
  0.0 941.2 jit_solution(12412474038883919479)
XLA Ops:
  8.1 6.3 all-to-all-start
  16.7 4.2 all-to-all-done
  21.6 7.6 multiply_reduce_fusion.11
  29.2 63.6 %psum.84 = f32[16]{0:T(128)S(1)} all-reduce(f32[16]{0:T(128)S(1)} %get-tuple-element.61), channel_id=1, replica_groups=mesh['patch'=16,'col'=8] {'patch','col'}, use_global_device_ids=true, to_apply=%region_2.0 | all-reduce | flops 16 | bytes 128 | tf_op jit(solution)/shard_map/psum | solution.py:94
  94.1 4.2 all-to-all-start.1
  98.3 4.8 collective-permute-start.3
  105.9 7.5 multiply_reduce_fusion.10
  113.4 66.1 %psum.85 = f32[16]{0:T(128)S(1)} all-reduce(f32[16]{0:T(128)S(1)} %get-tuple-element.63), channel_id=1, replica_groups=mesh['patch'=16,'col'=8] {'patch','col'}, use_global_device_ids=true, to_apply=%region_4.0 | all-reduce | flops 16 | bytes 128 | tf_op jit(solution)/shard_map/psum | solution.py:109
  179.7 63.2 %psum.86 = f32[16]{0:T(128)S(1)} all-reduce(f32[16]{0:T(128)S(1)} %multiply_reduce_fusion.9), channel_id=1, replica_groups=mesh['patch'=16,'col'=8] {'patch','col'}, use_global_device_ids=true, to_apply=%region_6.0 | all-reduce | flops 16 | bytes 128 | tf_op jit(solution)/shard_map/psum | solution.py:112
  244.1 4.2 all-to-all-start.2
  248.5 5.2 collective-permute-start.5
  255.9 7.5 multiply_reduce_fusion.8
  263.4 66.6 %psum.87 = f32[16]{0:T(128)S(1)} all-reduce(f32[16]{0:T(128)S(1)} %get-tuple-element.65), channel_id=1, replica_groups=mesh['patch'=16,'col'=8] {'patch','col'}, use_global_device_ids=true, to_apply=%region_8.0 | all-reduce | flops 16 | bytes 128 | tf_op jit(solution)/shard_map/psum | solution.py:109
  330.2 63.2 %psum.88 = f32[16]{0:T(128)S(1)} all-reduce(f32[16]{0:T(128)S(1)} %multiply_reduce_fusion.7), channel_id=1, replica_groups=mesh['patch'=16,'col'=8] {'patch','col'}, use_global_device_ids=true, to_apply=%region_10.0 | all-reduce | flops 16 | bytes 128 | tf_op jit(solution)/shard_map/psum | solution.py:109
  393.6 63.0 %psum.89 = f32[16]{0:T(128)S(1)} all-reduce(f32[16]{0:T(128)S(1)} %multiply_reduce_fusion.6), channel_id=1, replica_groups=mesh['patch'=16,'col'=8] {'patch','col'}, use_global_device_ids=true, to_apply=%region_12.0 | all-reduce | flops 16 | bytes 128 | tf_op jit(solution)/shard_map/psum | solution.py:112
  464.7 4.0 all-to-all-start.3
  469.3 4.2 collective-permute-start.7
  476.2 7.5 multiply_reduce_fusion.5
  483.7 66.1 %psum.90 = f32[16]{0:T(128)S(1)} all-reduce(f32[16]{0:T(128)S(1)} %get-tuple-element.67), channel_id=1, replica_groups=mesh['patch'=16,'col'=8] {'patch','col'}, use_global_device_ids=true, to_apply=%region_16.0 | all-reduce | flops 16 | bytes 128 | tf_op jit(solution)/shard_map/psum | solution.py:94
  551.1 4.2 all-to-all-start.4
  555.5 4.8 collective-permute-start.9
  562.9 7.5 multiply_reduce_fusion.4
  570.3 66.3 %psum.91 = f32[16]{0:T(128)S(1)} all-reduce(f32[16]{0:T(128)S(1)} %get-tuple-element.69), channel_id=1, replica_groups=mesh['patch'=16,'col'=8] {'patch','col'}, use_global_device_ids=true, to_apply=%region_18.0 | all-reduce | flops 16 | bytes 128 | tf_op jit(solution)/shard_map/psum | solution.py:109
  636.8 63.2 %psum.92 = f32[16]{0:T(128)S(1)} all-reduce(f32[16]{0:T(128)S(1)} %multiply_reduce_fusion.3), channel_id=1, replica_groups=mesh['patch'=16,'col'=8] {'patch','col'}, use_global_device_ids=true, to_apply=%region_20.0 | all-reduce | flops 16 | bytes 128 | tf_op jit(solution)/shard_map/psum | solution.py:112
  701.3 4.2 all-to-all-start.5
  705.5 4.8 collective-permute-start.11
  713.0 7.5 multiply_reduce_fusion.2
  720.5 66.1 %psum.93 = f32[16]{0:T(128)S(1)} all-reduce(f32[16]{0:T(128)S(1)} %get-tuple-element.71), channel_id=1, replica_groups=mesh['patch'=16,'col'=8] {'patch','col'}, use_global_device_ids=true, to_apply=%region_22.0 | all-reduce | flops 16 | bytes 128 | tf_op jit(solution)/shard_map/psum | solution.py:109
  786.8 63.2 %psum.94 = f32[16]{0:T(128)S(1)} all-reduce(f32[16]{0:T(128)S(1)} %multiply_reduce_fusion.1), channel_id=1, replica_groups=mesh['patch'=16,'col'=8] {'patch','col'}, use_global_device_ids=true, to_apply=%region_24.0 | all-reduce | flops 16 | bytes 128 | tf_op jit(solution)/shard_map/psum | solution.py:109
  850.2 63.3 %psum.95 = f32[16]{0:T(128)S(1)} all-reduce(f32[16]{0:T(128)S(1)} %multiply_reduce_fusion), channel_id=1, replica_groups=mesh['patch'=16,'col'=8] {'patch','col'}, use_global_device_ids=true, to_apply=%region_26.0 | all-reduce | flops 16 | bytes 128 | tf_op jit(solution)/shard_map/psum | solution.py:112
  926.0 4.2 collective-permute-start.13
  933.0 8.0 fusion.3
  (129 shorter events, 53.9 us)
Async XLA Ops:
  0.6 92.2 %copy-start = (f32[4,128,128]{2,1,0:T(8,128)S(1)}, f32[4,128,128]{2,1,0:T(8,128)}, u32[]{:S(2)}) copy-start(f32[4,128,128]{2,1,0:T(8,128)} %param.28) | copy-start | bytes 786436
  0.6 16.0 %collective-permute-start = (f32[4,16,128]{2,1,0:T(8,128)}, f32[4,16,128]{2,1,0:T(8,128)S(1)}, u32[]{:S(2)}, u32[]{:S(2)}) collective-permute-start(f32[4,16,128]{2,1,0:T(8,128)} %param.24), channel_id=1, source_target_pairs={{0,8},{8,16},{16,24},{24,32},{32,40},{40,48},{48,56},{56,64},{64,7... | collective-permute-start | bytes 98312 | tf_op jit(solution)/shard_map/ppermute | solution.py:15
  2.8 13.9 %collective-permute-start.1 = (f32[4,16,128]{2,1,0:T(8,128)}, f32[4,16,128]{2,1,0:T(8,128)S(1)}, u32[]{:S(2)}, u32[]{:S(2)}) collective-permute-start(f32[4,16,128]{2,1,0:T(8,128)} %param.24), channel_id=1, source_target_pairs={{0,120},{8,0},{16,8},{24,16},{32,24},{40,32},{48,40},{56,48},{64,5... | collective-permute-start | bytes 98312 | tf_op jit(solution)/shard_map/ppermute | solution.py:15
  8.1 12.8 %all-to-all-start = ((f32[8,4,16,128]{3,2,1,0:T(8,128)}), f32[8,4,16,128]{3,2,1,0:T(8,128)S(1)}, u32[]{:S(2)}, u32[]{:S(2)}) async-start(f32[8,4,16,128]{3,2,1,0:T(8,128)} %stack.42), calls=%async_computation | async-start | bytes 524288 | tf_op jit(solution)/shard_map/all_to_all | solution.py:63
  20.9 85.0 %copy-start.1 = (f32[4,16,128]{2,1,0:T(8,128)S(1)}, f32[4,16,128]{2,1,0:T(8,128)}, u32[]{:S(2)}) copy-start(f32[4,16,128]{2,1,0:T(8,128)} %param.24) | copy-start | bytes 98308
  20.9 85.0 %copy-start.4 = (f32[4,128]{1,0:T(4,128)S(1)}, f32[4,128]{1,0:T(4,128)}, u32[]{:S(2)}) copy-start(f32[4,128]{1,0:T(4,128)} %param.30) | copy-start | bytes 6148
  20.9 85.0 %copy-start.5 = (f32[4,128]{1,0:T(4,128)S(1)}, f32[4,128]{1,0:T(4,128)}, u32[]{:S(2)}) copy-start(f32[4,128]{1,0:T(4,128)} %param.29) | copy-start | bytes 6148
  20.9 85.0 %copy-start.6 = (f32[4,128]{1,0:T(4,128)S(1)}, f32[4,128]{1,0:T(4,128)}, u32[]{:S(2)}) copy-start(f32[4,128]{1,0:T(4,128)} %param.26) | copy-start | bytes 6148
  94.1 11.1 %all-to-all-start.1 = ((f32[8,4,16,128]{3,2,1,0:T(8,128)}), f32[8,4,16,128]{3,2,1,0:T(8,128)S(1)}, u32[]{:S(2)}, u32[]{:S(2)}) async-start(f32[8,4,16,128]{3,2,1,0:T(8,128)} %stack.43), calls=%async_computation.1 | async-start | bytes 524288 | tf_op jit(solution)/shard_map/all_to_all | solution.py:63
  98.3 6.1 collective-permute-start.2
  98.3 6.1 collective-permute-start.3
  244.1 11.1 %all-to-all-start.2 = ((f32[8,4,16,128]{3,2,1,0:T(8,128)}), f32[8,4,16,128]{3,2,1,0:T(8,128)S(1)}, u32[]{:S(2)}, u32[]{:S(2)}) async-start(f32[8,4,16,128]{3,2,1,0:T(8,128)} %stack.47), calls=%async_computation.2 | async-start | bytes 524288 | tf_op jit(solution)/shard_map/all_to_all | solution.py:63
  248.4 6.1 collective-permute-start.4
  248.5 6.2 collective-permute-start.5
  255.2 221.0 %copy-start.2 = (f32[4,16,128]{2,1,0:T(8,128)S(1)}, f32[4,16,128]{2,1,0:T(8,128)}, u32[]{:S(2)}) copy-start(f32[4,16,128]{2,1,0:T(8,128)} %param.25) | copy-start | bytes 98308
  464.7 10.8 %all-to-all-start.3 = ((f32[8,4,16,128]{3,2,1,0:T(8,128)}), f32[8,4,16,128]{3,2,1,0:T(8,128)S(1)}, u32[]{:S(2)}, u32[]{:S(2)}) async-start(f32[8,4,16,128]{3,2,1,0:T(8,128)} %stack.52), calls=%async_computation.3 | async-start | bytes 524288 | tf_op jit(solution)/shard_map/all_to_all | solution.py:63
  468.7 6.1 collective-permute-start.6
  469.3 5.5 collective-permute-start.7
  551.1 11.0 %all-to-all-start.4 = ((f32[8,4,16,128]{3,2,1,0:T(8,128)}), f32[8,4,16,128]{3,2,1,0:T(8,128)S(1)}, u32[]{:S(2)}, u32[]{:S(2)}) async-start(f32[8,4,16,128]{3,2,1,0:T(8,128)} %stack.53), calls=%async_computation.4 | async-start | bytes 524288 | tf_op jit(solution)/shard_map/all_to_all | solution.py:63
  555.3 6.2 collective-permute-start.8
  555.5 6.1 collective-permute-start.9
  701.3 11.1 %all-to-all-start.5 = ((f32[8,4,16,128]{3,2,1,0:T(8,128)}), f32[8,4,16,128]{3,2,1,0:T(8,128)S(1)}, u32[]{:S(2)}, u32[]{:S(2)}) async-start(f32[8,4,16,128]{3,2,1,0:T(8,128)} %stack.57), calls=%async_computation.5 | async-start | bytes 524288 | tf_op jit(solution)/shard_map/all_to_all | solution.py:63
  705.5 6.1 collective-permute-start.10
  705.5 6.1 collective-permute-start.11
  920.8 20.2 %copy-start.3 = (f32[4,16,128]{2,1,0:T(8,128)}, f32[4,16,128]{2,1,0:T(8,128)S(1)}, u32[]{:S(2)}) copy-start(f32[4,16,128]{2,1,0:T(8,128)S(1)} %add_add_fusion) | copy-start | bytes 98308
  921.5 10.8 %all-to-all-start.6 = ((f32[8,4,16,128]{3,2,1,0:T(8,128)}), f32[8,4,16,128]{3,2,1,0:T(8,128)S(1)}, u32[]{:S(2)}, u32[]{:S(2)}) async-start(f32[8,4,16,128]{3,2,1,0:T(8,128)} %stack.62), calls=%async_computation.6 | async-start | bytes 524288 | tf_op jit(solution)/shard_map/all_to_all | solution.py:63
  925.4 6.1 collective-permute-start.12
  926.0 5.5 collective-permute-start.13
